TPU v7x, 32 devices: a whole 2x2x4 slice. The times are simulated.
32 devices in a mesh: ctx: 8 (over z, y), fsdp: 4 (over x, core).
Axes of the slice: x: 2, y: 2, z: 4, core: 2. Of those that a mesh axis runs over, the one named last changes fastest.
Arguments:
- hidden_in: bfloat16 [4, 2048, 1536], P('fsdp', 'ctx'), may hold values from -6 to 6
- out_grad: bfloat16 [4, 2048, 1536], P('fsdp', 'ctx'), may hold values from -6 to 6
- positions: int32 [4, 2048], P('fsdp'), may hold values from 0 to 2047, as said below
- attn_gain: bfloat16 [1536], P('fsdp'), may hold values from 0.5 to 1.5
- w_query: bfloat16 [1536, 1536], P('fsdp'), may hold values from -0.15625 to 0.15625
- w_key: bfloat16 [1536, 768], P('fsdp'), may hold values from -0.15625 to 0.15625
- w_value: bfloat16 [1536, 768], P('fsdp'), may hold values from -0.15625 to 0.15625
- w_out: bfloat16 [1536, 1536], P('fsdp'), may hold values from -3 to 3
- ffn_gain: bfloat16 [1536], P('fsdp'), may hold values from 0.5 to 1.5
- w_gate: bfloat16 [1536, 4096], P('fsdp'), may hold values from -0.15625 to 0.15625
- w_up: bfloat16 [1536, 4096], P('fsdp'), may hold values from -0.15625 to 0.15625
- w_down: bfloat16 [1536, 4096], P('fsdp'), may hold values from -0.09375 to 0.09375
Outputs:
- out: bfloat16 [4, 2048, 1536], P('fsdp', 'ctx')
- input_grad: float32 [4, 2048, 1536], P('fsdp', 'ctx')
- attn_gain_grad: float32 [1536], P('fsdp')
- w_query_grad: float32 [1536, 1536], P('fsdp')
- w_key_grad: float32 [1536, 768], P('fsdp')
- w_value_grad: float32 [1536, 768], P('fsdp')
- w_out_grad: float32 [1536, 1536], P('fsdp')
- ffn_gain_grad: float32 [1536], P('fsdp')
- w_gate_grad: float32 [1536, 4096], P('fsdp')
- w_up_grad: float32 [1536, 4096], P('fsdp')
- w_down_grad: float32 [1536, 4096], P('fsdp')
Inputs may be any that keep to these rules, and one draw needn't show every extreme that they name: In each sequence, the 256 rows of one ctx index hold the positions of causal block b followed by those of block 15 - b, each in increasing order, where b is that index's place in a permutation of the 8 pairs drawn for that sequence; each sequence's positions are a permutation of 0 to 2047.
All inputs are finite; a program needn't handle non-finite values.
Results may differ from a plain program's by a relative error of at most 0.022.
Values may be sent and summed in bfloat16 or wider, within the bound.
No kernel may reach another device: no remote copies, remote signals or barrier semaphores. Data moves between devices by JAX's collectives and lax.ppermute only.
A program may use at most 448 MiB of HBM per device.

v0:
```python
import math
import jax
import jax.numpy as jnp
from jax import lax
from jax.sharding import PartitionSpec as P

HQ = 16
HK = 8
HD = 96
epsilon = 1e-05
rope_base = 100000.0
masked_score = -1e30


def angles_of(places):
    frequency = jnp.exp(jnp.arange(HD // 2, dtype=jnp.float32) * (-2.0 * math.log(rope_base) / HD))
    turned = places.astype(jnp.float32)[:, None] * frequency[None, :]
    return (jnp.cos(turned)[:, None, :], jnp.sin(turned)[:, None, :])


def rotate(values, cosine, sine):
    half_size = values.shape[-1] // 2
    first_half = values[..., :half_size]
    second_half = values[..., half_size:]
    return jnp.concatenate(
        [first_half * cosine - second_half * sine, second_half * cosine + first_half * sine],
        axis=-1,
    )


def contract_last(left, right):
    return lax.dot_general(
        left, right, (((1,), (1,)), ((), ())), preferred_element_type=jnp.float32
    )


def contract_first(left, right):
    return lax.dot_general(
        left, right, (((0,), (0,)), ((), ())), preferred_element_type=jnp.float32
    )


def rms_back(values, inverse, gain, grad_normed):
    weighted = gain * grad_normed
    inner = jnp.mean(values * weighted, axis=1, keepdims=True)
    grad_values = inverse * weighted - values * inverse * inverse * inverse * inner
    return (grad_values, jnp.sum(grad_normed * values * inverse, axis=0))


def body(
    hidden_in,
    out_grad,
    positions,
    attn_gain,
    w_query,
    w_key,
    w_value,
    w_out,
    ffn_gain,
    w_gate,
    w_up,
    w_down,
):
    shards = (attn_gain, w_query, w_key, w_value, w_out, ffn_gain, w_gate, w_up, w_down)
    weights = (
        lax.all_gather(shards[0], "fsdp", axis=0, tiled=True),
        lax.all_gather(shards[1], "fsdp", axis=0, tiled=True),
        lax.all_gather(shards[2], "fsdp", axis=0, tiled=True),
        lax.all_gather(shards[3], "fsdp", axis=0, tiled=True),
        lax.all_gather(shards[4], "fsdp", axis=0, tiled=True),
        lax.all_gather(shards[5], "fsdp", axis=0, tiled=True),
        lax.all_gather(shards[6], "fsdp", axis=0, tiled=True),
        lax.all_gather(shards[7], "fsdp", axis=0, tiled=True),
        lax.all_gather(shards[8], "fsdp", axis=0, tiled=True),
    )
    gain_one = weights[0].astype(jnp.float32)
    gain_two = weights[5].astype(jnp.float32)
    rows_in = hidden_in[0].astype(jnp.float32)
    row_count = rows_in.shape[0]
    group_size = HQ // HK
    scale = 1.0 / math.sqrt(HD)
    all_places = positions[0]
    own_places = lax.dynamic_slice_in_dim(
        all_places, lax.axis_index("ctx") * row_count, row_count, 0
    )
    cosine, sine = angles_of(own_places)
    inverse_one = lax.rsqrt(jnp.mean(rows_in * rows_in, axis=1, keepdims=True) + epsilon)
    normed_one = (rows_in * inverse_one * gain_one).astype(jnp.bfloat16)
    query = jnp.dot(normed_one, weights[1], preferred_element_type=jnp.float32)
    keys = jnp.dot(normed_one, weights[2], preferred_element_type=jnp.float32)
    values = jnp.dot(normed_one, weights[3], preferred_element_type=jnp.float32).astype(
        jnp.bfloat16
    )
    query_rot = (
        rotate(query.reshape(row_count, HQ, HD), cosine, sine)
        .astype(jnp.bfloat16)
        .reshape(row_count, HK, group_size, HD)
    )
    keys_rot = (
        rotate(keys.reshape(row_count, HK, HD), cosine, sine)
        .astype(jnp.bfloat16)
        .reshape(row_count, HK * HD)
    )
    keys_all, values_all = (
        lax.all_gather(keys_rot, "ctx", axis=0, tiled=True),
        lax.all_gather(values, "ctx", axis=0, tiled=True),
    )
    key_total = keys_all.shape[0]
    keys_all = keys_all.reshape(key_total, HK, HD)
    values_all = values_all.reshape(key_total, HK, HD)
    block_size = math.gcd(key_total, 512)
    block_count = key_total // block_size

    def scores_at(start):
        key_block = lax.dynamic_slice_in_dim(keys_all, start, block_size, 0)
        key_places = lax.dynamic_slice_in_dim(all_places, start, block_size, 0)
        raw = (
            jnp.einsum("rkgd,skd->rkgs", query_rot, key_block, preferred_element_type=jnp.float32)
            * scale
        )
        allowed = key_places[None, None, None, :] <= own_places[:, None, None, None]
        return (jnp.where(allowed, raw, masked_score), key_block)

    def running_total(block_index, carry):
        top_score, total = carry
        scores, unused = scores_at(block_index * block_size)
        new_top = jnp.maximum(top_score, jnp.max(scores, axis=-1))
        total = total * jnp.exp(top_score - new_top) + jnp.sum(
            jnp.exp(scores - new_top[..., None]), axis=-1
        )
        return (new_top, total)

    start_top = jnp.full((row_count, HK, group_size), masked_score, jnp.float32)
    start_total = jnp.zeros((row_count, HK, group_size), jnp.float32)
    top_score, total = lax.fori_loop(0, block_count, running_total, (start_top, start_total))
    log_total = top_score + jnp.log(total)

    def add_values(block_index, mixed):
        start = block_index * block_size
        scores, unused = scores_at(start)
        value_block = lax.dynamic_slice_in_dim(values_all, start, block_size, 0)
        soft = jnp.exp(scores - log_total[..., None]).astype(jnp.bfloat16)
        return mixed + jnp.einsum(
            "rkgs,skd->rkgd", soft, value_block, preferred_element_type=jnp.float32
        )

    mixed_exact = lax.fori_loop(
        0, block_count, add_values, jnp.zeros((row_count, HK, group_size, HD), jnp.float32)
    )
    mixed_low = mixed_exact.reshape(row_count, HQ * HD).astype(jnp.bfloat16)
    middle = rows_in + contract_last(mixed_low, weights[4])
    inverse_two = lax.rsqrt(jnp.mean(middle * middle, axis=1, keepdims=True) + epsilon)
    normed_two = (middle * inverse_two * gain_two).astype(jnp.bfloat16)
    gate = jnp.dot(normed_two, weights[6], preferred_element_type=jnp.float32)
    upward = jnp.dot(normed_two, weights[7], preferred_element_type=jnp.float32)
    sigmoid_gate = jax.nn.sigmoid(gate)
    swish = gate * sigmoid_gate
    hidden = (swish * upward).astype(jnp.bfloat16)
    result = (middle + contract_last(hidden, weights[8])).astype(jnp.bfloat16)
    weights = (
        lax.all_gather(shards[0], "fsdp", axis=0, tiled=True),
        lax.all_gather(shards[1], "fsdp", axis=0, tiled=True),
        lax.all_gather(shards[2], "fsdp", axis=0, tiled=True),
        lax.all_gather(shards[3], "fsdp", axis=0, tiled=True),
        lax.all_gather(shards[4], "fsdp", axis=0, tiled=True),
        lax.all_gather(shards[5], "fsdp", axis=0, tiled=True),
        lax.all_gather(shards[6], "fsdp", axis=0, tiled=True),
        lax.all_gather(shards[7], "fsdp", axis=0, tiled=True),
        lax.all_gather(shards[8], "fsdp", axis=0, tiled=True),
    )
    grad_down = out_grad[0]
    grad_hidden = jnp.dot(grad_down, weights[8], preferred_element_type=jnp.float32)
    grad_gate = (grad_hidden * upward * sigmoid_gate * (1.0 + gate * (1.0 - sigmoid_gate))).astype(
        jnp.bfloat16
    )
    grad_up = (grad_hidden * swish).astype(jnp.bfloat16)
    grad_normed_two = contract_last(grad_gate, weights[6]) + contract_last(grad_up, weights[7])
    grad_middle_norm, grad_gain_two = rms_back(middle, inverse_two, gain_two, grad_normed_two)
    grad_middle = grad_down.astype(jnp.float32) + grad_middle_norm
    grad_branch = grad_middle.astype(jnp.bfloat16)
    grad_mixed = jnp.dot(grad_branch, weights[4], preferred_element_type=jnp.float32).astype(
        jnp.bfloat16
    )
    grad_mixed = grad_mixed.reshape(row_count, HK, group_size, HD)
    delta = jnp.sum(grad_mixed.astype(jnp.float32) * mixed_exact, axis=-1)

    def key_step(block_index, carry):
        grad_query, grad_keys, grad_values = carry
        start = block_index * block_size
        scores, key_block = scores_at(start)
        value_block = lax.dynamic_slice_in_dim(values_all, start, block_size, 0)
        soft = jnp.exp(scores - log_total[..., None])
        grad_soft = jnp.einsum(
            "rkgd,skd->rkgs", grad_mixed, value_block, preferred_element_type=jnp.float32
        )
        grad_scores = (soft * (grad_soft - delta[..., None])).astype(jnp.bfloat16)
        grad_query = grad_query + scale * jnp.einsum(
            "rkgs,skd->rkgd", grad_scores, key_block, preferred_element_type=jnp.float32
        )
        key_part = scale * jnp.einsum(
            "rkgs,rkgd->skd", grad_scores, query_rot, preferred_element_type=jnp.float32
        )
        value_part = jnp.einsum(
            "rkgs,rkgd->skd",
            soft.astype(jnp.bfloat16),
            grad_mixed,
            preferred_element_type=jnp.float32,
        )
        grad_keys = lax.dynamic_update_slice_in_dim(
            grad_keys, key_part.reshape(block_size, HK * HD), start, 0
        )
        grad_values = lax.dynamic_update_slice_in_dim(
            grad_values, value_part.reshape(block_size, HK * HD), start, 0
        )
        return (grad_query, grad_keys, grad_values)

    start_query = jnp.zeros((row_count, HK, group_size, HD), jnp.float32)
    start_keys = jnp.zeros((key_total, HK * HD), jnp.float32)
    grad_query, grad_keys, grad_values = lax.fori_loop(
        0, block_count, key_step, (start_query, start_keys, start_keys)
    )
    own_key_grads, own_value_grads = (
        lax.psum_scatter(
            grad_keys.astype(jnp.bfloat16), "ctx", scatter_dimension=0, tiled=True
        ).astype(jnp.float32),
        lax.psum_scatter(
            grad_values.astype(jnp.bfloat16), "ctx", scatter_dimension=0, tiled=True
        ).astype(jnp.float32),
    )
    grad_keys_raw = (
        rotate(own_key_grads.reshape(row_count, HK, HD), cosine, -sine)
        .reshape(row_count, HK * HD)
        .astype(jnp.bfloat16)
    )
    grad_values_low = own_value_grads.astype(jnp.bfloat16)
    grad_query_raw = (
        rotate(grad_query.reshape(row_count, HQ, HD), cosine, -sine)
        .reshape(row_count, HQ * HD)
        .astype(jnp.bfloat16)
    )
    grad_normed_one = (
        contract_last(grad_query_raw, weights[1])
        + contract_last(grad_keys_raw, weights[2])
        + contract_last(grad_values_low, weights[3])
    )
    grad_rows_norm, grad_gain_one = rms_back(rows_in, inverse_one, gain_one, grad_normed_one)
    input_grad = (grad_middle + grad_rows_norm)[None]
    down_part = lax.psum_scatter(
        contract_first(grad_down, hidden).astype(jnp.bfloat16),
        "fsdp",
        scatter_dimension=0,
        tiled=True,
    )
    gate_part, up_part, out_part, gain_two_part = (
        lax.psum_scatter(
            contract_first(normed_two, grad_gate).astype(jnp.bfloat16),
            "fsdp",
            scatter_dimension=0,
            tiled=True,
        ).astype(jnp.float32),
        lax.psum_scatter(
            contract_first(normed_two, grad_up).astype(jnp.bfloat16),
            "fsdp",
            scatter_dimension=0,
            tiled=True,
        ).astype(jnp.float32),
        lax.psum_scatter(
            contract_first(grad_branch, mixed_low).astype(jnp.bfloat16),
            "fsdp",
            scatter_dimension=0,
            tiled=True,
        ).astype(jnp.float32),
        lax.psum_scatter(
            grad_gain_two.astype(jnp.bfloat16), "fsdp", scatter_dimension=0, tiled=True
        ).astype(jnp.float32),
    )
    query_part, key_part, value_part, gain_one_part = (
        lax.psum_scatter(
            contract_first(normed_one, grad_query_raw).astype(jnp.bfloat16),
            "fsdp",
            scatter_dimension=0,
            tiled=True,
        ).astype(jnp.float32),
        lax.psum_scatter(
            contract_first(normed_one, grad_keys_raw).astype(jnp.bfloat16),
            "fsdp",
            scatter_dimension=0,
            tiled=True,
        ).astype(jnp.float32),
        lax.psum_scatter(
            contract_first(normed_one, grad_values_low).astype(jnp.bfloat16),
            "fsdp",
            scatter_dimension=0,
            tiled=True,
        ).astype(jnp.float32),
        lax.psum_scatter(
            grad_gain_one.astype(jnp.bfloat16), "fsdp", scatter_dimension=0, tiled=True
        ).astype(jnp.float32),
    )
    summed = (
        lax.psum(gain_one_part.astype(jnp.bfloat16), "ctx").astype(jnp.float32),
        lax.psum(query_part.astype(jnp.bfloat16), "ctx").astype(jnp.float32),
        lax.psum(key_part.astype(jnp.bfloat16), "ctx").astype(jnp.float32),
        lax.psum(value_part.astype(jnp.bfloat16), "ctx").astype(jnp.float32),
        lax.psum(out_part.astype(jnp.bfloat16), "ctx").astype(jnp.float32),
        lax.psum(gain_two_part.astype(jnp.bfloat16), "ctx").astype(jnp.float32),
        lax.psum(gate_part.astype(jnp.bfloat16), "ctx").astype(jnp.float32),
        lax.psum(up_part.astype(jnp.bfloat16), "ctx").astype(jnp.float32),
        lax.psum(down_part, "ctx").astype(jnp.float32),
    )
    return (
        result[None],
        input_grad,
        summed[0],
        summed[1],
        summed[2],
        summed[3],
        summed[4],
        summed[5],
        summed[6],
        summed[7],
        summed[8],
    )


def solution(mesh):
    placed = (
        P("fsdp", "ctx", None),
        P("fsdp", "ctx", None),
        P("fsdp", None),
        P("fsdp"),
        P("fsdp", None),
        P("fsdp", None),
        P("fsdp", None),
        P("fsdp", None),
        P("fsdp"),
        P("fsdp", None),
        P("fsdp", None),
        P("fsdp", None),
    )
    return jax.shard_map(
        body,
        mesh=mesh,
        in_specs=placed,
        out_specs=(
            P("fsdp", "ctx", None),
            P("fsdp", "ctx", None),
            P("fsdp"),
            P("fsdp", None),
            P("fsdp", None),
            P("fsdp", None),
            P("fsdp", None),
            P("fsdp"),
            P("fsdp", None),
            P("fsdp", None),
            P("fsdp", None),
        ),
        check_vma=False,
    )
```

profile of v0, /device:TPU:0, one launch (start us, length us, event | category | flops | bytes accessed | tf_op | source)
XLA Modules:
  0.0 1717.1 jit_solution(11761543956456879321)
XLA Ops:
  15.9 20.5 %all-gather.12.cloned.1.call-done = bf16[1536,768]{1,0:T(8,128)(2,1)} async-done(((bf16[384,768]{1,0:T(8,128)(2,1)}), bf16[1536,768]{1,0:T(8,128)(2,1)}) %all-gather.12.cloned.1.call-update) | async-done | bytes 2359312 | tf_op jit(solution)/shard_map/all_gather | solution.py:69
  40.7 21.4 %all-gather.16.cloned.1.call-done = bf16[1536,768]{1,0:T(8,128)(2,1)} async-done(((bf16[384,768]{1,0:T(8,128)(2,1)}), bf16[1536,768]{1,0:T(8,128)(2,1)}) %all-gather.16.cloned.1.call-update) | async-done | bytes 2359312 | tf_op jit(solution)/shard_map/all_gather | solution.py:68
  75.4 25.8 %all-gather.20.cloned.1.call-done = bf16[1536,1536]{1,0:T(8,128)(2,1)} async-done(((bf16[384,1536]{1,0:T(8,128)(2,1)}), bf16[1536,1536]{1,0:T(8,128)(2,1)}) %all-gather.20.cloned.1.call-update) | async-done | bytes 4718608 | tf_op jit(solution)/shard_map/all_gather | solution.py:67
  112.0 52.3 %all-gather.14.cloned.1.call-done = bf16[2048,768]{1,0:T(8,128)(2,1)} async-done(((bf16[256,768]{1,0:T(8,128)(2,1)}), bf16[2048,768]{1,0:T(8,128)(2,1)}) %all-gather.14.cloned.1.call-update) | async-done | bytes 3145744 | tf_op jit(solution)/shard_map/all_gather | solution.py:106
  168.9 59.5 %all-gather.18.cloned.1.call-done = bf16[2048,768]{0,1:T(8,128)(2,1)} async-done(((bf16[256,768]{0,1:T(8,128)(2,1)}), bf16[2048,768]{0,1:T(8,128)(2,1)}) %all-gather.18.cloned.1.call-update) | async-done | bytes 3145744 | tf_op jit(solution)/shard_map/all_gather | solution.py:105
  228.4 46.4 %while.48 = (s32[]{:T(128)}, f32[256,8,2]{0,2,1:T(2,128)S(1)}, f32[256,8,2]{0,2,1:T(2,128)S(1)}, s32[2048]{0:T(1024)S(1)}, s32[256]{0:T(256)S(1)}, /*index=5*/bf...) while((s32[]{:T(128)}, f32[256,8,2]{0,2,1:T(2,128)S(1)}, ...), condition=%wide.region_4.5_spmd.clone, body=%wide.region_1.4_spmd.clone.sunk | while | flops 417484800 | bytes 18963636 | solution.py:135
  274.9 24.7 %while.49 = (s32[]{:T(128)}, f32[256,8,2,96]{0,3,2,1:T(8,128)}, bf16[2048,8,96]{0,2,1:T(8,128)(2,1)}, s32[2048]{0:T(1024)S(1)}, s32[256]{0:T(256)S(1)}, /*index=...) while((s32[]{:T(128)}, f32[256,8,2,96]{0,3,2,1:T(8,128)}, ...), condition=%wide.region_6.7_spmd.clone, body=%wide.region_5.6_spmd.clone.sunk | while | flops 814612480 | bytes 5792440 | solution.py:147
  307.4 41.8 %all-gather.24.cloned.1.call-done = bf16[1536,4096]{1,0:T(8,128)(2,1)} async-done(((bf16[384,4096]{1,0:T(8,128)(2,1)}), bf16[1536,4096]{1,0:T(8,128)(2,1)}) %all-gather.24.cloned.1.call-update) | async-done | bytes 12582928 | tf_op jit(solution)/shard_map/all_gather | solution.py:72
  349.2 9.5 fusion.87
  358.7 74.2 %all-gather.26.cloned.1.call-done = bf16[1536,4096]{1,0:T(8,128)(2,1)} async-done(((bf16[384,4096]{1,0:T(8,128)(2,1)}), bf16[1536,4096]{1,0:T(8,128)(2,1)}) %all-gather.26.cloned.1.call-update) | async-done | bytes 12582928 | tf_op jit(solution)/shard_map/all_gather | solution.py:73
  432.9 9.7 fusion.88
  442.6 74.1 %all-gather.28.cloned.1.call-done = bf16[1536,4096]{1,0:T(8,128)(2,1)} async-done(((bf16[384,4096]{1,0:T(8,128)(2,1)}), bf16[1536,4096]{1,0:T(8,128)(2,1)}) %all-gather.28.cloned.1.call-update) | async-done | bytes 12582928 | tf_op jit(solution)/shard_map/all_gather | solution.py:74
  516.7 10.8 multiply_convert_fusion
  527.4 8.0 fusion.89
  535.5 7.5 multiply_reduce_fusion
  557.5 84.5 %while.50 = (s32[]{:T(128)}, f32[256,8,2,96]{0,3,2,1:T(8,128)S(1)}, bf16[2048,768]{0,1:T(8,128)(2,1)}, bf16[2048,768]{0,1:T(8,128)(2,1)}, bf16[2048,8,96]{0,2,1:...) while((s32[]{:T(128)}, f32[256,8,2,96]{0,3,2,1:T(8,128)S(1)}, ...), condition=%wide.region_11.12_spmd.clone, body=%wide.region_10.11_spmd.clone.sunk | while | flops 2036334592 | bytes 141745520 | solution.py:219
  643.2 8.5 fusion.47
  651.7 16.9 copy.65
  680.7 36.3 %reduce-scatter.12.cloned.1.call-done = bf16[256,768]{0,1:T(8,128)(2,1)} async-done(((bf16[2048,768]{0,1:T(8,128)(2,1)}), bf16[256,768]{0,1:T(8,128)(2,1)}) %reduce-scatter.12.cloned.1.call-update) | async-done | bytes 393232 | tf_op jit(solution)/shard_map/reduce_scatter | solution.py:223
  720.6 74.2 %reduce-scatter.14.cloned.1.call-done = bf16[256,768]{0,1:T(8,128)(2,1)} async-done(((bf16[2048,768]{0,1:T(8,128)(2,1)}), bf16[256,768]{0,1:T(8,128)(2,1)}) %reduce-scatter.14.cloned.1.call-update) | async-done | bytes 393232 | tf_op jit(solution)/shard_map/reduce_scatter | solution.py:226
  798.2 9.7 convolution_convert_fusion.2
  808.0 9.4 convolution_convert_fusion.1
  817.6 77.9 %reduce-scatter.28.cloned.1.call-done = bf16[384,4096]{1,0:T(8,128)(2,1)} async-done(((bf16[1536,4096]{1,0:T(8,128)(2,1)}), bf16[384,4096]{1,0:T(8,128)(2,1)}) %reduce-scatter.28.cloned.1.call-update) | async-done | bytes 3145744
  900.2 46.4 %reduce-scatter.16.cloned.1.call-done = bf16[384,1536]{1,0:T(8,128)(2,1)} async-done(((bf16[1536,1536]{1,0:T(8,128)(2,1)}), bf16[384,1536]{1,0:T(8,128)(2,1)}) %reduce-scatter.16.cloned.1.call-update) | async-done | bytes 1179664 | tf_op jit(solution)/shard_map/reduce_scatter | solution.py:278
  946.5 51.0 %reduce-scatter.22.cloned.1.call-done = bf16[384,1536]{1,0:T(8,128)(2,1)} async-done(((bf16[1536,1536]{1,0:T(8,128)(2,1)}), bf16[384,1536]{1,0:T(8,128)(2,1)}) %reduce-scatter.22.cloned.1.call-update) | async-done | bytes 1179664 | tf_op jit(solution)/shard_map/reduce_scatter | solution.py:267
  997.5 36.0 %reduce-scatter.18.cloned.1.call-done = bf16[384,768]{1,0:T(8,128)(2,1)} async-done(((bf16[1536,768]{1,0:T(8,128)(2,1)}), bf16[384,768]{1,0:T(8,128)(2,1)}) %reduce-scatter.18.cloned.1.call-update) | async-done | bytes 589840 | tf_op jit(solution)/shard_map/reduce_scatter | solution.py:284
  1033.6 36.2 %reduce-scatter.20.cloned.1.call-done = bf16[384,768]{1,0:T(8,128)(2,1)} async-done(((bf16[1536,768]{1,0:T(8,128)(2,1)}), bf16[384,768]{1,0:T(8,128)(2,1)}) %reduce-scatter.20.cloned.1.call-update) | async-done | bytes 589840 | tf_op jit(solution)/shard_map/reduce_scatter | solution.py:290
  1069.8 101.5 %reduce-scatter.24.cloned.1.call-done = bf16[384,4096]{1,0:T(8,128)(2,1)} async-done(((bf16[1536,4096]{1,0:T(8,128)(2,1)}), bf16[384,4096]{1,0:T(8,128)(2,1)}) %reduce-scatter.24.cloned.1.call-update) | async-done | bytes 3145744 | tf_op jit(solution)/shard_map/reduce_scatter | solution.py:255
  1171.3 101.6 %reduce-scatter.26.cloned.1.call-done = bf16[384,4096]{1,0:T(8,128)(2,1)} async-done(((bf16[1536,4096]{1,0:T(8,128)(2,1)}), bf16[384,4096]{1,0:T(8,128)(2,1)}) %reduce-scatter.26.cloned.1.call-update) | async-done | bytes 3145744 | tf_op jit(solution)/shard_map/reduce_scatter | solution.py:261
  1278.8 7.7 fusion.50
  1296.9 22.7 %all-reduce.2 = (bf16[384]{0:T(512)(128)(2,1)S(1)}, bf16[384]{0:T(512)(128)(2,1)S(1)}) all-reduce(bf16[384]{0:T(512)(128)(2,1)S(1)} %dynamic-slice.2, bf16[384]{0:T(512)(128)(2,1)S(1)} %dynamic-slice.4), channel_id=1, replica_groups=mesh['ctx'=8,'fsdp'=4] {'ctx'}, use_global_device_ids=true, to_apply=%region_17.18 | all-reduce | flops 768 | bytes 3072 | tf_op jit(solution)/shard_map/psum | solution.py:301
  1323.9 369.0 %all-reduce.7.cloned.1.call-done = (bf16[384,4096]{0,1:T(8,128)(2,1)}, bf16[384,1536]{1,0:T(8,128)(2,1)}, bf16[384,768]{1,0:T(8,128)(2,1)}, bf16[384,768]{1,0:T(...) async-done(((bf16[384,4096]{0,1:T(8,128)(2,1)}, bf16[384,1536]{1,0:T(8,128)(2,1)}, bf16[384,768]{1,0:T(8,128)(2,1)}, ...) | async-done | bytes 12976144 | tf_op jit(solution)/shard_map/psum | solution.py:309
  (289 shorter events, 281.0 us)
Async XLA Ops:
  7.2 8.4 copy-start.3
  7.2 29.2 %all-gather.12.cloned.1.call-start = ((), (), s32[]{:S(2)}) async-start(), calls=%async_computation.9 | async-start | bytes 2949120 | tf_op jit(solution)/shard_map/all_gather | solution.py:69
  7.9 54.1 %all-gather.16.cloned.1.call-start = ((), (), s32[]{:S(2)}) async-start(), calls=%async_computation.11 | async-start | bytes 2949120 | tf_op jit(solution)/shard_map/all_gather | solution.py:68
  8.7 92.5 %all-gather.20.cloned.1.call-start = ((), (), s32[]{:S(2)}) async-start(), calls=%async_computation.13 | async-start | bytes 5898240 | tf_op jit(solution)/shard_map/all_gather | solution.py:67
  9.4 154.8 %all-gather.14.cloned.1.call-start = ((), (), s32[]{:S(2)}) async-start(), calls=%async_computation.10 | async-start | bytes 3538944 | tf_op jit(solution)/shard_map/all_gather | solution.py:106
  15.6 92.1 %copy-start.30 = (f32[1536]{0:T(1024)}, f32[1536]{0:T(1024)S(1)}, u32[]{:S(2)}) copy-start(f32[1536]{0:T(1024)S(1)} %reshape.350) | copy-start | bytes 18436
  15.9 91.9 %copy-start.34 = (f32[256]{0:T(256)}, f32[256]{0:T(256)S(1)}, u32[]{:S(2)}) copy-start(f32[256]{0:T(256)S(1)} %add_rsqrt_fusion.1) | copy-start | bytes 3076
  15.9 23.8 %copy-start.33 = (s32[1,2048]{1,0:T(1,128)S(1)}, s32[1,2048]{1,0:T(1,128)}, u32[]{:S(2)}) copy-start(s32[1,2048]{1,0:T(1,128)} %param.20) | copy-start | bytes 24580
  39.7 188.7 %all-gather.18.cloned.1.call-start = ((), (), s32[]{:S(2)}) async-start(), calls=%async_computation.12 | async-start | bytes 3538944 | tf_op jit(solution)/shard_map/all_gather | solution.py:105
  40.7 71.0 %copy-start.25 = (f32[256,48]{0,1:T(8,128)}, f32[256,48]{0,1:T(8,128)S(1)}, u32[]{:S(2)}) copy-start(f32[256,48]{0,1:T(8,128)S(1)} %get-tuple-element.719) | copy-start | bytes 147460
  66.7 235.2 %all-gather.22.cloned.1.call-start = ((), (), s32[]{:S(2)}) async-start(), calls=%async_computation.14 | async-start | bytes 5898240 | tf_op jit(solution)/shard_map/all_gather | solution.py:70
  67.3 281.9 %all-gather.24.cloned.1.call-start = ((), (), s32[]{:S(2)}) async-start(), calls=%async_computation.15 | async-start | bytes 15728640 | tf_op jit(solution)/shard_map/all_gather | solution.py:72
  68.0 364.9 %all-gather.26.cloned.1.call-start = ((), (), s32[]{:S(2)}) async-start(), calls=%async_computation.16 | async-start | bytes 15728640 | tf_op jit(solution)/shard_map/all_gather | solution.py:73
  68.8 447.9 %all-gather.28.cloned.1.call-start = ((), (), s32[]{:S(2)}) async-start(), calls=%async_computation.17 | async-start | bytes 15728640 | tf_op jit(solution)/shard_map/all_gather | solution.py:74
  69.5 647.4 %reduce-scatter.12.cloned.1.call-start = ((), (), s32[]{:S(2)}) async-start(), calls=%async_computation.18 | async-start | bytes 3538944 | tf_op jit(solution)/shard_map/reduce_scatter | solution.py:223
  527.4 8.0 copy-start.23
  527.4 8.1 copy-start.22
  527.4 8.1 copy-start.9
  535.5 7.6 copy-start.12
  557.8 5.7 copy-start.16
  599.9 5.7 copy-start.16
  621.0 5.7 copy-start.16
  642.1 152.7 %reduce-scatter.14.cloned.1.call-start = ((), (), s32[]{:S(2)}) async-start(), calls=%async_computation.19 | async-start | bytes 3538944 | tf_op jit(solution)/shard_map/reduce_scatter | solution.py:226
  642.9 252.7 %reduce-scatter.28.cloned.1.call-start = ((), (), s32[]{:S(2)}) async-start(), calls=%async_computation.26 | async-start | bytes 15728640
  668.7 277.8 %reduce-scatter.16.cloned.1.call-start = ((), (), s32[]{:S(2)}) async-start(), calls=%async_computation.20 | async-start | bytes 5898240 | tf_op jit(solution)/shard_map/reduce_scatter | solution.py:278
  674.4 323.1 %reduce-scatter.22.cloned.1.call-start = ((), (), s32[]{:S(2)}) async-start(), calls=%async_computation.23 | async-start | bytes 5898240 | tf_op jit(solution)/shard_map/reduce_scatter | solution.py:267
  680.6 353.0 %reduce-scatter.18.cloned.1.call-start = ((), (), s32[]{:S(2)}) async-start(), calls=%async_computation.21 | async-start | bytes 2949120 | tf_op jit(solution)/shard_map/reduce_scatter | solution.py:284
  720.6 349.2 %reduce-scatter.20.cloned.1.call-start = ((), (), s32[]{:S(2)}) async-start(), calls=%async_computation.22 | async-start | bytes 2949120 | tf_op jit(solution)/shard_map/reduce_scatter | solution.py:290
  798.2 373.2 %reduce-scatter.24.cloned.1.call-start = ((), (), s32[]{:S(2)}) async-start(), calls=%async_computation.24 | async-start | bytes 15728640 | tf_op jit(solution)/shard_map/reduce_scatter | solution.py:255
  808.0 464.9 %reduce-scatter.26.cloned.1.call-start = ((), (), s32[]{:S(2)}) async-start(), calls=%async_computation.25 | async-start | bytes 15728640 | tf_op jit(solution)/shard_map/reduce_scatter | solution.py:261
  817.4 875.5 %all-reduce.7.cloned.1.call-start = ((), (), s32[]{:S(2)}) async-start(), calls=%async_computation.27 | async-start | bytes 25952256 | tf_op jit(solution)/shard_map/psum | solution.py:309
  1278.8 7.7 copy-start.7
  (42 other events, 118.6 us)
Sparse Core Ops, SparseCore 0:
  9.6 26.7 all-gather.11
  37.9 24.0 all-gather.15
  63.6 37.4 all-gather.19
  103.7 60.4 all-gather.13
  166.7 61.6 all-gather.17
  229.8 35.6 all-gather.21
  267.1 82.0 all-gather.23
  350.8 82.0 all-gather.25
  434.5 82.1 all-gather.27
  642.2 74.7 reduce-scatter.11
  720.6 74.1 reduce-scatter.13
  797.3 98.2 reduce-scatter.27
  898.7 47.8 reduce-scatter.15
  949.7 47.8 reduce-scatter.21
  1000.5 33.0 reduce-scatter.17
  1036.7 33.0 reduce-scatter.19
  1072.2 99.0 reduce-scatter.23
  1173.8 99.0 reduce-scatter.25
  1279.2 413.6 all-reduce.6
where the time goes:
time: 1720 us
  waiting for transfers between devices  1310 us (76%)
  matrix products  226 us (13%)
  local copies, waits for them, and re-layouts  77.4 us (5%)
  other arithmetic  50.7 us (3%)
  blocking collectives  40.9 us (2%)
    psum x1, waiting for transfers between devices, body(): lax.psum(down_part, 'ctx').astype(jnp.float32)  369 us
    reduce_scatter x1, waiting for transfers between devices, body(): lax.psum_scatter(contract_first(normed_two, grad_up).astype(jnp.bfloat16)...  102 us
    reduce_scatter x1, waiting for transfers between devices, body(): lax.psum_scatter(contract_first(normed_two, grad_gate).astype(jnp.bfloat1...  102 us
    unnamed x20, waiting for transfers between devices  83.4 us
    reduce_scatter x1, waiting for transfers between devices, body(): lax.psum_scatter(grad_values.astype(jnp.bfloat16), 'ctx', scatter_dimensi...  74.2 us
    all_gather x1, waiting for transfers between devices, body(): lax.all_gather(shards[7], 'fsdp', axis=0, tiled=True)  74.2 us
    all_gather x1, waiting for transfers between devices, body(): lax.all_gather(shards[8], 'fsdp', axis=0, tiled=True)  74.1 us
    all_gather x1, waiting for transfers between devices, body(): lax.all_gather(keys_rot, 'ctx', axis=0, tiled=True)  59.5 us
  transfers between devices with their start and end apart: 19, of which 18 were waited for; matrix products, arithmetic and copies ran while one was open for 12% of the time, Pallas kernels for 0%

commit v1 on v0

--- a/solution.py
+++ b/solution.py
@@ -306,7 +306,7 @@
         lax.psum(gain_two_part.astype(jnp.bfloat16), "ctx").astype(jnp.float32),
         lax.psum(gate_part.astype(jnp.bfloat16), "ctx").astype(jnp.float32),
         lax.psum(up_part.astype(jnp.bfloat16), "ctx").astype(jnp.float32),
-        lax.psum(down_part, "ctx").astype(jnp.float32),
+        jnp.sum(lax.all_gather(down_part, "ctx"), axis=0).astype(jnp.float32),
     )
     return (
         result[None],

time: 1720 us -> 2170 us (1.26)
  waiting for transfers between devices: 1310 us -> 1670 us
  other arithmetic: 50.7 us -> 106 us
  local copies, waits for them, and re-layouts: 77.4 us -> 101 us
    all_gather x0 -> x1, waiting for transfers between devices: none -> 468 us  [body(): lax.all_gather(down_part, 'ctx')]
    psum x1, waiting for transfers between devices: 369 us -> 261 us  [body(): lax.psum(query_part.astype(jnp.bfloat16), 'ctx').astype(jnp.float32)]
    reduce_sum x0 -> x1, other arithmetic: none -> 54.2 us  [body(): jnp.sum(lax.all_gather(down_part, 'ctx'), axis=0).astype(jnp.float32)]
    reduce_scatter x1, waiting for transfers between devices: 46.4 us -> 3.37 us  [body(): lax.psum_scatter(contract_first(normed_one, grad_query_raw).astype(jnp.bf...]
    reduce_scatter x1, waiting for transfers between devices: 36.3 us -> 63.5 us  [body(): lax.psum_scatter(grad_keys.astype(jnp.bfloat16), 'ctx', scatter_dimension...]
    unnamed x78 -> x79, local copies, waits for them, and re-layouts: 32.7 us -> 56.2 us
    unnamed x20 -> x21, waiting for transfers between devices: 83.4 us -> 107 us
  transfers between devices with their start and end apart: 19 -> 20, of which waited for: 18 -> 19; matrix products, arithmetic and copies ran while one was open for 12% -> 10% of each run, Pallas kernels for 0% -> 0%
where the time goes in v1:
time: 2170 us; the launch traced here: 2160 us
  waiting for transfers between devices  1670 us (77%)
  matrix products  225 us (10%)
  other arithmetic  106 us (5%)
  local copies, waits for them, and re-layouts  101 us (5%)
  blocking collectives  40.6 us (2%)
    all_gather x1, waiting for transfers between devices, body(): lax.all_gather(down_part, 'ctx')  468 us
    psum x1, waiting for transfers between devices, body(): lax.psum(query_part.astype(jnp.bfloat16), 'ctx').astype(jnp.float32)  261 us
    unnamed x21, waiting for transfers between devices  107 us
    reduce_scatter x1, waiting for transfers between devices, body(): lax.psum_scatter(contract_first(normed_two, grad_up).astype(jnp.bfloat16)...  102 us
    reduce_scatter x1, waiting for transfers between devices, body(): lax.psum_scatter(contract_first(normed_two, grad_gate).astype(jnp.bfloat1...  102 us
    reduce_scatter x1, waiting for transfers between devices, body(): lax.psum_scatter(grad_values.astype(jnp.bfloat16), 'ctx', scatter_dimensi...  74.1 us
    all_gather x1, waiting for transfers between devices, body(): lax.all_gather(shards[8], 'fsdp', axis=0, tiled=True)  73.3 us
    all_gather x1, waiting for transfers between devices, body(): lax.all_gather(shards[7], 'fsdp', axis=0, tiled=True)  73.3 us
  transfers between devices with their start and end apart: 20, of which 19 were waited for; matrix products, arithmetic and copies ran while one was open for 10% of the time, Pallas kernels for 0%

profile of v1, /device:TPU:0, one launch (start us, length us, event | category | flops | bytes accessed | tf_op | source)
XLA Modules:
  0.0 2160.9 jit_solution(14000730596208613637)
XLA Ops:
  15.9 20.5 all-gather.14.cloned.1.call-done
  40.6 21.4 all-gather.18.cloned.1.call-done
  74.8 26.3 %all-gather.22.cloned.1.call-done = bf16[1536,1536]{1,0:T(8,128)(2,1)} async-done(((bf16[384,1536]{1,0:T(8,128)(2,1)}), bf16[1536,1536]{1,0:T(8,128)(2,1)}) %all-gather.22.cloned.1.call-update) | async-done | bytes 4718608 | tf_op jit(solution)/shard_map/all_gather | solution.py:67
  111.9 52.3 %all-gather.16.cloned.1.call-done = bf16[2048,768]{1,0:T(8,128)(2,1)} async-done(((bf16[256,768]{1,0:T(8,128)(2,1)}), bf16[2048,768]{1,0:T(8,128)(2,1)}) %all-gather.16.cloned.1.call-update) | async-done | bytes 3145744 | tf_op jit(solution)/shard_map/all_gather | solution.py:106
  168.8 59.5 %all-gather.20.cloned.1.call-done = bf16[2048,768]{0,1:T(8,128)(2,1)} async-done(((bf16[256,768]{0,1:T(8,128)(2,1)}), bf16[2048,768]{0,1:T(8,128)(2,1)}) %all-gather.20.cloned.1.call-update) | async-done | bytes 3145744 | tf_op jit(solution)/shard_map/all_gather | solution.py:105
  228.4 46.4 %while.48 = (s32[]{:T(128)}, f32[256,8,2]{0,2,1:T(2,128)S(1)}, f32[256,8,2]{0,2,1:T(2,128)S(1)}, s32[2048]{0:T(1024)S(1)}, s32[256]{0:T(256)S(1)}, /*index=5*/bf...) while((s32[]{:T(128)}, f32[256,8,2]{0,2,1:T(2,128)S(1)}, ...), condition=%wide.region_4.5_spmd.clone, body=%wide.region_1.4_spmd.clone.sunk | while | flops 417484800 | bytes 18963636 | solution.py:135
  274.9 24.8 %while.49 = (s32[]{:T(128)}, f32[256,8,2,96]{0,3,2,1:T(8,128)}, bf16[2048,8,96]{0,2,1:T(8,128)(2,1)}, s32[2048]{0:T(1024)S(1)}, s32[256]{0:T(256)S(1)}, /*index=...) while((s32[]{:T(128)}, f32[256,8,2,96]{0,3,2,1:T(8,128)}, ...), condition=%wide.region_6.7_spmd.clone, body=%wide.region_5.6_spmd.clone.sunk | while | flops 814612480 | bytes 5792440 | solution.py:147
  308.4 40.7 %all-gather.26.cloned.1.call-done = bf16[1536,4096]{1,0:T(8,128)(2,1)} async-done(((bf16[384,4096]{1,0:T(8,128)(2,1)}), bf16[1536,4096]{1,0:T(8,128)(2,1)}) %all-gather.26.cloned.1.call-update) | async-done | bytes 12582928 | tf_op jit(solution)/shard_map/all_gather | solution.py:72
  349.2 10.4 fusion.87
  359.6 73.3 %all-gather.28.cloned.1.call-done = bf16[1536,4096]{1,0:T(8,128)(2,1)} async-done(((bf16[384,4096]{1,0:T(8,128)(2,1)}), bf16[1536,4096]{1,0:T(8,128)(2,1)}) %all-gather.28.cloned.1.call-update) | async-done | bytes 12582928 | tf_op jit(solution)/shard_map/all_gather | solution.py:73
  432.9 10.4 fusion.88
  443.3 73.3 %all-gather.30.cloned.1.call-done = bf16[1536,4096]{1,0:T(8,128)(2,1)} async-done(((bf16[384,4096]{1,0:T(8,128)(2,1)}), bf16[1536,4096]{1,0:T(8,128)(2,1)}) %all-gather.30.cloned.1.call-update) | async-done | bytes 12582928 | tf_op jit(solution)/shard_map/all_gather | solution.py:74
  516.6 10.7 multiply_convert_fusion
  557.8 84.6 %while.50 = (s32[]{:T(128)}, f32[256,8,2,96]{0,3,2,1:T(8,128)S(1)}, bf16[2048,768]{0,1:T(8,128)(2,1)}, bf16[2048,768]{0,1:T(8,128)(2,1)}, bf16[2048,8,96]{0,2,1:...) while((s32[]{:T(128)}, f32[256,8,2,96]{0,3,2,1:T(8,128)S(1)}, ...), condition=%wide.region_11.12_spmd.clone, body=%wide.region_10.11_spmd.clone.sunk | while | flops 2036334592 | bytes 141745520 | solution.py:219
  653.9 63.5 %reduce-scatter.12.cloned.1.call-done = bf16[256,768]{0,1:T(8,128)(2,1)} async-done(((bf16[2048,768]{0,1:T(8,128)(2,1)}), bf16[256,768]{0,1:T(8,128)(2,1)}) %reduce-scatter.12.cloned.1.call-update) | async-done | bytes 393232 | tf_op jit(solution)/shard_map/reduce_scatter | solution.py:223
  721.1 74.1 %reduce-scatter.14.cloned.1.call-done = bf16[256,768]{0,1:T(8,128)(2,1)} async-done(((bf16[2048,768]{0,1:T(8,128)(2,1)}), bf16[256,768]{0,1:T(8,128)(2,1)}) %reduce-scatter.14.cloned.1.call-update) | async-done | bytes 393232 | tf_op jit(solution)/shard_map/reduce_scatter | solution.py:226
  798.5 9.3 convolution_convert_fusion.2
  807.9 8.1 convolution_convert_fusion.1
  817.3 8.2 fusion.47
  825.5 16.1 copy.63
  845.0 51.2 %reduce-scatter.22.cloned.1.call-done = bf16[384,1536]{1,0:T(8,128)(2,1)} async-done(((bf16[1536,1536]{1,0:T(8,128)(2,1)}), bf16[384,1536]{1,0:T(8,128)(2,1)}) %reduce-scatter.22.cloned.1.call-update) | async-done | bytes 1179664 | tf_op jit(solution)/shard_map/reduce_scatter | solution.py:267
  896.2 36.1 %reduce-scatter.18.cloned.1.call-done = bf16[384,768]{1,0:T(8,128)(2,1)} async-done(((bf16[1536,768]{1,0:T(8,128)(2,1)}), bf16[384,768]{1,0:T(8,128)(2,1)}) %reduce-scatter.18.cloned.1.call-update) | async-done | bytes 589840 | tf_op jit(solution)/shard_map/reduce_scatter | solution.py:284
  932.3 36.2 %reduce-scatter.20.cloned.1.call-done = bf16[384,768]{1,0:T(8,128)(2,1)} async-done(((bf16[1536,768]{1,0:T(8,128)(2,1)}), bf16[384,768]{1,0:T(8,128)(2,1)}) %reduce-scatter.20.cloned.1.call-update) | async-done | bytes 589840 | tf_op jit(solution)/shard_map/reduce_scatter | solution.py:290
  968.5 101.5 %reduce-scatter.24.cloned.1.call-done = bf16[384,4096]{1,0:T(8,128)(2,1)} async-done(((bf16[1536,4096]{1,0:T(8,128)(2,1)}), bf16[384,4096]{1,0:T(8,128)(2,1)}) %reduce-scatter.24.cloned.1.call-update) | async-done | bytes 3145744 | tf_op jit(solution)/shard_map/reduce_scatter | solution.py:255
  1070.0 101.5 %reduce-scatter.26.cloned.1.call-done = bf16[384,4096]{1,0:T(8,128)(2,1)} async-done(((bf16[1536,4096]{1,0:T(8,128)(2,1)}), bf16[384,4096]{1,0:T(8,128)(2,1)}) %reduce-scatter.26.cloned.1.call-update) | async-done | bytes 3145744 | tf_op jit(solution)/shard_map/reduce_scatter | solution.py:261
  1171.8 101.3 %reduce-scatter.28.cloned.1.call-done = bf16[384,4096]{1,0:T(8,128)(2,1)} async-done(((bf16[1536,4096]{1,0:T(8,128)(2,1)}), bf16[384,4096]{1,0:T(8,128)(2,1)}) %reduce-scatter.28.cloned.1.call-update) | async-done | bytes 3145744
  1283.6 8.3 fusion.50
  1302.6 22.8 %all-reduce.2 = (bf16[384]{0:T(512)(128)(2,1)S(1)}, bf16[384]{0:T(512)(128)(2,1)S(1)}) all-reduce(bf16[384]{0:T(512)(128)(2,1)S(1)} %dynamic-slice.2, bf16[384]{0:T(512)(128)(2,1)S(1)} %dynamic-slice.4), channel_id=1, replica_groups=mesh['ctx'=8,'fsdp'=4] {'ctx'}, use_global_device_ids=true, to_apply=%region_17.18 | all-reduce | flops 768 | bytes 3072 | tf_op jit(solution)/shard_map/psum | solution.py:301
  1329.6 261.4 %all-reduce.7.cloned.1.call-done = (bf16[384,1536]{1,0:T(8,128)(2,1)}, bf16[384,768]{1,0:T(8,128)(2,1)}, bf16[384,768]{1,0:T(8,128)(2,1)}, bf16[384,1536]{1,0:T(...) async-done(((bf16[384,1536]{1,0:T(8,128)(2,1)}, bf16[384,768]{1,0:T(8,128)(2,1)}, bf16[384,768]{1,0:T(8,128)(2,1)}, bf16[384,1536]{1,0:T(8,128)(2,1)}, ...) | async-done | bytes 9830416 | tf_op jit(solution)/shard_map/psum | solution.py:302
  1605.0 467.5 %all-gather.32.cloned.1.call-done = bf16[3072,4096]{0,1:T(8,128)(2,1)} async-done(((bf16[384,4096]{0,1:T(8,128)(2,1)}), bf16[3072,4096]{0,1:T(8,128)(2,1)}) %all-gather.32.cloned.1.call-update) | async-done | bytes 25165840 | tf_op jit(solution)/shard_map/all_gather | solution.py:309
  2072.5 23.3 %copy.65 = bf16[512,8,8,384]{3,2,1,0:T(8,128)(2,1)} copy(bf16[512,8,8,384]{3,1,2,0:T(8,128)(2,1)} %bitcast.262) | data formatting | bytes 50331648
  2095.8 54.2 %bitcast_reduce_fusion = bf16[384,4096]{0,1:T(8,128)(2,1)S(1)} fusion(bf16[512,8,8,384]{3,2,1,0:T(8,128)(2,1)} %copy.65), kind=kLoop, calls=%fused_computation.54 | loop fusion | flops 11010048 | bytes 28311552 | tf_op jit(solution)/shard_map/reduce_sum | solution.py:309
  (294 shorter events, 300.7 us)
Async XLA Ops:
  7.2 8.4 copy-start.3
  7.2 29.2 %all-gather.14.cloned.1.call-start = ((), (), s32[]{:S(2)}) async-start(), calls=%async_computation.9 | async-start | bytes 2949120 | tf_op jit(solution)/shard_map/all_gather | solution.py:69
  7.9 54.1 %all-gather.18.cloned.1.call-start = ((), (), s32[]{:S(2)}) async-start(), calls=%async_computation.11 | async-start | bytes 2949120 | tf_op jit(solution)/shard_map/all_gather | solution.py:68
  8.7 92.4 %all-gather.22.cloned.1.call-start = ((), (), s32[]{:S(2)}) async-start(), calls=%async_computation.13 | async-start | bytes 5898240 | tf_op jit(solution)/shard_map/all_gather | solution.py:67
  9.4 154.8 %all-gather.16.cloned.1.call-start = ((), (), s32[]{:S(2)}) async-start(), calls=%async_computation.10 | async-start | bytes 3538944 | tf_op jit(solution)/shard_map/all_gather | solution.py:106
  15.6 92.1 %copy-start.30 = (f32[1536]{0:T(1024)}, f32[1536]{0:T(1024)S(1)}, u32[]{:S(2)}) copy-start(f32[1536]{0:T(1024)S(1)} %reshape.351) | copy-start | bytes 18436
  15.9 91.9 %copy-start.34 = (f32[256]{0:T(256)}, f32[256]{0:T(256)S(1)}, u32[]{:S(2)}) copy-start(f32[256]{0:T(256)S(1)} %add_rsqrt_fusion.1) | copy-start | bytes 3076
  15.9 23.8 %copy-start.33 = (s32[1,2048]{1,0:T(1,128)S(1)}, s32[1,2048]{1,0:T(1,128)}, u32[]{:S(2)}) copy-start(s32[1,2048]{1,0:T(1,128)} %param.20) | copy-start | bytes 24580
  39.7 188.7 %all-gather.20.cloned.1.call-start = ((), (), s32[]{:S(2)}) async-start(), calls=%async_computation.12 | async-start | bytes 3538944 | tf_op jit(solution)/shard_map/all_gather | solution.py:105
  40.6 71.0 %copy-start.25 = (f32[256,48]{0,1:T(8,128)}, f32[256,48]{0,1:T(8,128)S(1)}, u32[]{:S(2)}) copy-start(f32[256,48]{0,1:T(8,128)S(1)} %get-tuple-element.696) | copy-start | bytes 147460
  66.7 235.4 %all-gather.24.cloned.1.call-start = ((), (), s32[]{:S(2)}) async-start(), calls=%async_computation.14 | async-start | bytes 5898240 | tf_op jit(solution)/shard_map/all_gather | solution.py:70
  67.3 281.9 %all-gather.26.cloned.1.call-start = ((), (), s32[]{:S(2)}) async-start(), calls=%async_computation.15 | async-start | bytes 15728640 | tf_op jit(solution)/shard_map/all_gather | solution.py:72
  68.0 364.8 %all-gather.28.cloned.1.call-start = ((), (), s32[]{:S(2)}) async-start(), calls=%async_computation.16 | async-start | bytes 15728640 | tf_op jit(solution)/shard_map/all_gather | solution.py:73
  68.8 447.8 %all-gather.30.cloned.1.call-start = ((), (), s32[]{:S(2)}) async-start(), calls=%async_computation.17 | async-start | bytes 15728640 | tf_op jit(solution)/shard_map/all_gather | solution.py:74
  69.5 647.9 %reduce-scatter.12.cloned.1.call-start = ((), (), s32[]{:S(2)}) async-start(), calls=%async_computation.18 | async-start | bytes 3538944 | tf_op jit(solution)/shard_map/reduce_scatter | solution.py:223
  527.3 8.0 copy-start.23
  527.3 8.0 copy-start.22
  527.3 8.0 copy-start.9
  535.4 7.9 copy-start.12
  557.8 5.8 copy-start.16
  642.4 152.7 %reduce-scatter.14.cloned.1.call-start = ((), (), s32[]{:S(2)}) async-start(), calls=%async_computation.19 | async-start | bytes 3538944 | tf_op jit(solution)/shard_map/reduce_scatter | solution.py:226
  643.2 201.9 %reduce-scatter.16.cloned.1.call-start = ((), (), s32[]{:S(2)}) async-start(), calls=%async_computation.20 | async-start | bytes 5898240 | tf_op jit(solution)/shard_map/reduce_scatter | solution.py:278
  648.4 247.8 %reduce-scatter.22.cloned.1.call-start = ((), (), s32[]{:S(2)}) async-start(), calls=%async_computation.23 | async-start | bytes 5898240 | tf_op jit(solution)/shard_map/reduce_scatter | solution.py:267
  653.8 278.5 %reduce-scatter.18.cloned.1.call-start = ((), (), s32[]{:S(2)}) async-start(), calls=%async_computation.21 | async-start | bytes 2949120 | tf_op jit(solution)/shard_map/reduce_scatter | solution.py:284
  721.0 77.5 %copy-start.7 = (bf16[256,1536]{1,0:T(8,128)(2,1)S(1)}, bf16[256,1536]{1,0:T(8,128)(2,1)}, u32[]{:S(2)}) copy-start(bf16[256,1536]{1,0:T(8,128)(2,1)} %multiply_convert_fusion.3) | copy-start | bytes 2359300
  721.0 247.5 %reduce-scatter.20.cloned.1.call-start = ((), (), s32[]{:S(2)}) async-start(), calls=%async_computation.22 | async-start | bytes 2949120 | tf_op jit(solution)/shard_map/reduce_scatter | solution.py:290
  798.5 271.5 %reduce-scatter.24.cloned.1.call-start = ((), (), s32[]{:S(2)}) async-start(), calls=%async_computation.24 | async-start | bytes 15728640 | tf_op jit(solution)/shard_map/reduce_scatter | solution.py:255
  807.8 363.7 %reduce-scatter.26.cloned.1.call-start = ((), (), s32[]{:S(2)}) async-start(), calls=%async_computation.25 | async-start | bytes 15728640 | tf_op jit(solution)/shard_map/reduce_scatter | solution.py:261
  816.0 457.1 %reduce-scatter.28.cloned.1.call-start = ((), (), s32[]{:S(2)}) async-start(), calls=%async_computation.27 | async-start | bytes 15728640
  841.6 749.4 %all-reduce.7.cloned.1.call-start = ((), (), s32[]{:S(2)}) async-start(), calls=%async_computation.28 | async-start | bytes 19660800 | tf_op jit(solution)/shard_map/psum | solution.py:302
  1171.6 900.9 %all-gather.32.cloned.1.call-start = ((), (), s32[]{:S(2)}) async-start(), calls=%async_computation.26 | async-start | bytes 28311552 | tf_op jit(solution)/shard_map/all_gather | solution.py:309
  1283.6 8.3 copy-start.6
  (43 other events, 126.4 us)
Sparse Core Ops, SparseCore 0:
  9.6 26.7 all-gather.13
  37.9 24.0 all-gather.17
  63.6 37.4 all-gather.21
  103.7 60.4 all-gather.15
  166.7 61.6 all-gather.19
  229.8 35.6 all-gather.23
  267.0 82.0 all-gather.25
  350.7 82.0 all-gather.27
  434.4 82.0 all-gather.29
  642.5 74.8 reduce-scatter.11
  721.0 74.0 reduce-scatter.13
  798.1 46.9 reduce-scatter.15
  848.3 47.8 reduce-scatter.21
  899.2 33.0 reduce-scatter.17
  935.4 33.0 reduce-scatter.19
  970.9 99.0 reduce-scatter.23
  1072.5 99.0 reduce-scatter.25
  1174.0 99.0 reduce-scatter.27
  1278.4 312.6 all-reduce.6
  1593.1 479.3 all-gather.31
